TPU v7x, 128 devices: a whole 4x4x4 slice. The times are simulated.
128 devices in a mesh: slot: 16 (over y, z), head: 2 (over x_lo), conv: 4 (over x_hi, core).
Axes of the slice: x: 4 (x_hi: 2, x_lo: 2; x = x_hi * 2 + x_lo), y: 4, z: 4, core: 2. Of those that a mesh axis runs over, the one named last changes fastest.
Arguments:
- queries: bfloat16 [1024, 64, 128], P(('conv', 'slot'), 'head'), may hold values from -96 to 96
- out_grad: bfloat16 [1024, 64, 128], P(('conv', 'slot'), 'head'), may hold values from -768 to 768
- row_positions: int32 [1024], P('conv'), may hold values from 0 to 8191
- slot_offsets: int32 [16384], P('slot'), may hold values from 0 to 16382, as said below
- cache: float32 [2, 16384, 4, 128], P(None, 'slot', 'head'), may hold values from -12 to 12
- first_moment: float32 [2, 16384, 4, 128], P(None, 'slot', 'head'), may hold values from -6 to 6
- second_moment: float32 [2, 16384, 4, 128], P(None, 'slot', 'head'), may hold values from 0.01 to 1000
Outputs:
- new_cache: float32 [2, 16384, 4, 128], P(None, 'slot', 'head')
- new_first_moment: float32 [2, 16384, 4, 128], P(None, 'slot', 'head')
- new_second_moment: float32 [2, 16384, 4, 128], P(None, 'slot', 'head')
- query_grad: float32 [1024, 64, 128], P(('conv', 'slot'), 'head')
Inputs may be any that keep to these rules, and one draw needn't show every extreme that they name: `slot_offsets`: never falls from one slot to the next; its first two entries are 0.
All inputs are finite; a program needn't handle non-finite values.
Results may differ from a plain program's by a relative error of at most 0.012.
The roundings to bfloat16 on the way count: a program that leaves them out, or rounds other values in their place, can miss the bound.
Values may be sent and summed in bfloat16 or wider, within the bound.
A program may use at most 128 MiB of HBM per device.

v0:
```python
import math
import jax
import jax.numpy as jnp
from jax import lax
from jax.sharding import PartitionSpec as P

STEP = 20
learn_rate = 0.01
beta_one = 0.9
beta_two = 0.95
adam_eps = 1e-08
masked_score = -1e30


def merged(x, axis, combine):
    everything = jax.tree.map(lambda part: lax.all_gather(part, axis), x)
    leading = jax.tree.map(lambda part: part[0], everything)

    def lap(k, so_far):
        return combine(so_far, jax.tree.map(lambda part: part[k], everything))

    return lax.fori_loop(1, lax.axis_size(axis), lap, leading)


def merge_pairs(earlier, later):
    largest = jnp.maximum(earlier[0], later[0])
    return (
        largest,
        earlier[1] * jnp.exp(earlier[0] - largest) + later[1] * jnp.exp(later[0] - largest),
    )


def local(queries, out_grad, row_positions, slot_offsets, cache, first_moment, second_moment):
    query_all, grad_all = (
        lax.all_gather(queries, "slot", axis=0, tiled=True),
        lax.all_gather(out_grad, "slot", axis=0, tiled=True),
    )
    total_rows, head_count, head_width = query_all.shape
    kv_count = cache.shape[2]
    group_heads = head_count // kv_count
    score_scale = 1.0 / math.sqrt(head_width)
    block_rows = min(64, total_rows)
    block_count = total_rows // block_rows
    key_half = cache[0].astype(jnp.bfloat16)
    value_half = cache[1].astype(jnp.bfloat16)
    query_blocks = query_all.reshape(block_count, block_rows, kv_count, group_heads, head_width)
    grad_blocks = grad_all.reshape(block_count, block_rows, kv_count, group_heads, head_width)
    visible_all = (slot_offsets[None, :] <= row_positions[:, None]).reshape(
        block_count, block_rows, -1
    )

    def masked_scores(query_block, visible):
        raw_score = (
            jnp.einsum("rkgd,skd->rkgs", query_block, key_half, preferred_element_type=jnp.float32)
            * score_scale
        )
        return jnp.where(visible[:, None, None, :], raw_score, masked_score)

    def weights_from(scores, visible, offset):
        return jnp.where(visible[:, None, None, :], jnp.exp(scores - offset[..., None]), 0.0)

    def gradient_products(grad_block):
        return jnp.einsum(
            "rkgd,skd->rkgs", grad_block, value_half, preferred_element_type=jnp.float32
        )

    def max_pass(inputs):
        query_block, visible = inputs
        scores = masked_scores(query_block, visible)
        largest = jnp.max(scores, axis=-1)
        return (largest, jnp.sum(weights_from(scores, visible, largest), axis=-1))

    largest, denominator = lax.map(max_pass, (query_blocks, visible_all))
    largest, denominator = merged((largest, denominator), "slot", merge_pairs)
    log_total = largest + jnp.log(denominator)

    def product_pass(inputs):
        query_block, grad_block, visible, block_total = inputs
        probability = weights_from(masked_scores(query_block, visible), visible, block_total)
        return jnp.sum(probability * gradient_products(grad_block), axis=-1)

    partial_sum = lax.map(product_pass, (query_blocks, grad_blocks, visible_all, log_total))
    row_sum = lax.psum(partial_sum, "slot")

    def last_pass(running, inputs):
        key_grad, value_grad = running
        query_block, grad_block, visible, block_total, block_sum = inputs
        probability = weights_from(masked_scores(query_block, visible), visible, block_total)
        prob_grad = gradient_products(grad_block)
        score_grad = (probability * (prob_grad - block_sum[..., None])).astype(jnp.bfloat16)
        prob_half = probability.astype(jnp.bfloat16)
        value_grad = value_grad + jnp.einsum(
            "rkgs,rkgd->skd", prob_half, grad_block, preferred_element_type=jnp.float32
        )
        key_grad = (
            key_grad
            + jnp.einsum(
                "rkgs,rkgd->skd", score_grad, query_block, preferred_element_type=jnp.float32
            )
            * score_scale
        )
        query_part = (
            jnp.einsum("rkgs,skd->rkgd", score_grad, key_half, preferred_element_type=jnp.float32)
            * score_scale
        )
        return ((key_grad, value_grad), query_part)

    empty_grad = jnp.zeros(key_half.shape, jnp.float32)
    (key_grad, value_grad), query_parts = lax.scan(
        last_pass,
        (empty_grad, empty_grad),
        (query_blocks, grad_blocks, visible_all, log_total, row_sum),
    )
    query_terms = query_parts.reshape(total_rows, head_count, head_width)
    summed = lax.psum(query_terms, "slot")
    own_rows = queries.shape[0]
    query_grad = lax.dynamic_slice_in_dim(summed, lax.axis_index("slot") * own_rows, own_rows, 0)
    key_total, value_total = lax.psum((key_grad, value_grad), "conv")
    slot_grad = jnp.stack([key_total, value_total])
    new_first = beta_one * first_moment + (1.0 - beta_one) * slot_grad
    new_second = beta_two * second_moment + (1.0 - beta_two) * slot_grad * slot_grad
    first_fix = 1.0 - beta_one**STEP
    second_fix = 1.0 - beta_two**STEP
    new_cache = cache - learn_rate * (new_first / first_fix) / (
        jnp.sqrt(new_second / second_fix) + adam_eps
    )
    return (new_cache, new_first, new_second, query_grad)


def solution(mesh):
    in_specs = (
        P(("conv", "slot"), "head", None),
        P(("conv", "slot"), "head", None),
        P("conv"),
        P("slot"),
        P(None, "slot", "head", None),
        P(None, "slot", "head", None),
        P(None, "slot", "head", None),
    )
    out_specs = (
        P(None, "slot", "head", None),
        P(None, "slot", "head", None),
        P(None, "slot", "head", None),
        P(("conv", "slot"), "head", None),
    )
    return jax.shard_map(local, mesh=mesh, in_specs=in_specs, out_specs=out_specs, check_vma=False)
```

profile of v0, /device:TPU:1, one launch (start us, length us, event | category | flops | bytes accessed | tf_op | source)
XLA Modules:
  0.0 525.3 jit_solution(10511550598650439508)
XLA Ops:
  9.5 1.8 copy.70
  13.1 43.8 %all-gather.5.cloned.1.call-done = bf16[256,32,128]{2,1,0:T(8,128)(2,1)} async-done(((bf16[16,32,128]{2,1,0:T(8,128)(2,1)}), bf16[256,32,128]{2,1,0:T(8,128)(2,1)}) %all-gather.5.cloned.1.call-update) | async-done | bytes 2097168 | tf_op jit(solution)/shard_map/all_gather | solution.py:35
  56.9 3.3 copy.50
  60.1 43.2 %all-gather.7.cloned.1.call-done = bf16[256,32,128]{2,1,0:T(8,128)(2,1)} async-done(((bf16[16,32,128]{2,1,0:T(8,128)(2,1)}), bf16[256,32,128]{2,1,0:T(8,128)(2,1)}) %all-gather.7.cloned.1.call-update) | async-done | bytes 2097168 | tf_op jit(solution)/shard_map/all_gather | solution.py:36
  103.3 3.3 copy.51
  106.6 23.2 %while.54 = (s32[]{:T(128)}, f32[4,64,2,16]{1,3,2,0:T(8,128)S(1)}, f32[4,64,2,16]{1,3,2,0:T(8,128)S(1)}, pred[4,64,1024]{2,1,0:T(8,128)(4,1)S(1)}, bf16[4,64,2,1...) while((s32[]{:T(128)}, f32[4,64,2,16]{1,3,2,0:T(8,128)S(1)}, ...), condition=%wide.region_3.4_spmd, body=%wide.region_0.3_spmd.sunk | while | flops 553644032 | bytes 18210912 | solution.py:73
  106.6 2.8 bitcast_reduce_fusion.2
  109.4 2.8 fusion.87
  112.4 2.8 bitcast_reduce_fusion.2
  115.2 2.8 fusion.87
  118.2 2.8 bitcast_reduce_fusion.2
  121.0 2.8 fusion.87
  124.0 2.8 bitcast_reduce_fusion.2
  126.8 2.8 fusion.87
  129.8 19.1 %all-gather.1 = f32[64,64,2,16]{1,3,2,0:T(8,128)S(1)} all-gather(f32[4,64,2,16]{1,3,2,0:T(8,128)S(1)} %get-tuple-element.272), channel_id=3, replica_groups=mesh['slot'=16,'head'=2,'conv'=4] {'slot'}, dimensions={0}, use_global_device_ids=true | all-gather | bytes 557056 | tf_op jit(solution)/shard_map/all_gather | solution.py:16
  148.9 17.4 %all-gather = f32[64,64,2,16]{1,3,2,0:T(8,128)S(1)} all-gather(f32[4,64,2,16]{1,3,2,0:T(8,128)S(1)} %get-tuple-element.271), channel_id=2, replica_groups=mesh['slot'=16,'head'=2,'conv'=4] {'slot'}, dimensions={0}, use_global_device_ids=true | all-gather | bytes 557056 | tf_op jit(solution)/shard_map/all_gather | solution.py:16
  166.3 1.0 copy-done.4
  167.2 13.9 %while.55 = (s32[]{:T(128)}, f32[4,64,2,16]{1,3,2,0:T(8,128)S(1)}, f32[4,64,2,16]{1,3,2,0:T(8,128)S(1)}, f32[16,4,64,2,16]{2,4,3,1,0:T(8,128)}, f32[16,4,64,2,16...) while((s32[]{:T(128)}, f32[4,64,2,16]{1,3,2,0:T(8,128)S(1)}, f32[4,64,2,16]{1,3,2,0:T(8,128)S(1)}, ...), condition=%wide.region_5.6_spmd, body=%wide.region_4.5_spmd.sunk | while | flops 49157 | bytes 196731 | solution.py:22
  168.1 0.9 fusion.88
  169.1 0.9 fusion.88
  170.0 0.9 fusion.88
  181.5 31.2 %while.56 = (s32[]{:T(128)}, f32[4,64,2,16]{3,1,2,0:T(8,128)}, pred[4,64,1024]{2,1,0:T(8,128)(4,1)S(1)}, bf16[4,64,2,16,128]{4,3,1,2,0:T(8,128)(2,1)}, bf16[1024...) while((s32[]{:T(128)}, f32[4,64,2,16]{3,1,2,0:T(8,128)}, ...), condition=%wide.region_8.9_spmd, body=%wide.region_6.8_spmd.sunk | while | flops 1086322688 | bytes 21397652 | solution.py:82
  181.5 2.4 fusion.93
  183.9 4.7 fusion.94
  189.4 2.4 fusion.93
  191.7 4.7 fusion.94
  197.1 2.4 fusion.93
  199.5 4.7 fusion.94
  204.9 2.4 fusion.93
  207.3 4.7 fusion.94
  212.7 61.1 %psum.28 = f32[4,64,2,16]{3,1,2,0:T(8,128)S(1)} all-reduce(f32[4,64,2,16]{3,1,2,0:T(8,128)} %get-tuple-element.275), channel_id=1, replica_groups=mesh['slot'=16,'head'=2,'conv'=4] {'slot'}, use_global_device_ids=true, to_apply=%region_9.10 | all-reduce | flops 8192 | bytes 65536 | tf_op jit(solution)/shard_map/psum | solution.py:83
  273.8 52.7 %while.57 = (s32[]{:T(128)}, f32[1024,2,128]{0,2,1:T(8,128)S(1)}, f32[1024,2,128]{0,2,1:T(8,128)S(1)}, f32[4,64,2,16,128]{4,3,2,1,0:T(8,128)}, bf16[4,64,2,16,12...) while((s32[]{:T(128)}, f32[1024,2,128]{0,2,1:T(8,128)S(1)}, ...), condition=%wide.region_11.12_spmd.clone, body=%wide.region_10.11_spmd.clone.sunk | while | flops 2711093248 | bytes 59867360 | solution.py:109
  273.9 2.4 fusion.105
  276.4 2.7 fusion.108
  279.1 3.5 fusion.106
  282.5 2.1 fusion.107
  284.7 1.2 fusion.109
  285.9 1.1 copy_dynamic-update-slice_fusion.2
  287.1 2.4 fusion.105
  289.6 2.7 fusion.108
  292.2 3.5 fusion.106
  295.7 2.1 fusion.107
  297.8 1.2 fusion.109
  299.1 1.2 copy_dynamic-update-slice_fusion.2
  300.3 2.4 fusion.105
  302.7 2.7 fusion.108
  305.4 3.5 fusion.106
  308.9 2.1 fusion.107
  311.0 1.2 fusion.109
  312.3 1.1 copy_dynamic-update-slice_fusion.2
  313.4 2.4 fusion.105
  315.9 2.7 fusion.108
  318.6 3.5 fusion.106
  322.1 2.1 fusion.107
  324.2 1.2 fusion.109
  325.4 1.1 copy_dynamic-update-slice_fusion.2
  326.6 1.3 copy.52
  327.9 1.3 copy.53
  329.7 81.8 %all-reduce.6.cloned.1.call-done = (f32[1,1024,2,128]{3,2,1,0:T(2,128)}, f32[1,1024,2,128]{3,2,1,0:T(2,128)}) async-done(((f32[1,1024,2,128]{3,2,1,0:T(2,128)}, f32[1,1024,2,128]{3,2,1,0:T(2,128)}), (f32[1,1024,2,128]{3,2,1,0:T(2,128)}, f32[1,1024,2,128]{3,2,1,0:T(2,128)})) %all-reduce.6.cloned.1.call-update) | async-done | bytes 2097168 | tf_op jit(solution)/shard_map/psum | solution.py:118
  411.5 1.4 constant_dynamic-update-slice_fusion.3
  413.0 1.5 constant_dynamic-update-slice_fusion.2
  414.5 8.0 %divide_subtract_fusion = (f32[2,1024,2,128]{3,2,1,0:T(2,128)}, f32[2,1024,2,128]{3,2,1,0:T(2,128)}, f32[2,1024,2,128]{3,2,1,0:T(2,128)}) fusion(f32[2,1024,2,128]{3,2,1,0:T(2,128)S(1)} %copy-done, f32[2,1024,2,128]{3,2,1,0:T(2,128)S(1)} %constant_dynamic-update-slice_fusion.2, f32[2,1024,2,128]{3,2,1,0:T(2,128)S(1)} %copy-done.1, ...), kind=kLoop, calls=%fused_computation.80 | loop fusion | flops 6291456 | bytes 14680064 | tf_op jit(solution)/shard_map/sub | solution.py:124
  422.5 94.6 %all-reduce.4.cloned.1.call-done = f32[256,32,128]{2,1,0:T(8,128)} async-done(((f32[256,32,128]{2,1,0:T(8,128)}), f32[256,32,128]{2,1,0:T(8,128)}) %all-reduce.4.cloned.1.call-update) | async-done | bytes 4194320 | tf_op jit(solution)/shard_map/psum | solution.py:115
  517.1 1.7 constant_dynamic-slice_fusion
  (103 shorter events, 19.2 us)
Async XLA Ops:
  7.2 49.7 %all-gather.5.cloned.1.call-start = ((), (), s32[]{:S(2)}) async-start(), calls=%async_computation | async-start | bytes 2228224 | tf_op jit(solution)/shard_map/all_gather | solution.py:35
  7.9 95.4 %all-gather.7.cloned.1.call-start = ((), (), s32[]{:S(2)}) async-start(), calls=%async_computation.1 | async-start | bytes 2228224 | tf_op jit(solution)/shard_map/all_gather | solution.py:36
  8.6 402.9 %all-reduce.6.cloned.1.call-start = ((), (), s32[]{:S(2)}) async-start(), calls=%async_computation.3 | async-start | bytes 4194304 | tf_op jit(solution)/shard_map/psum | solution.py:118
  166.2 1.0 copy-start.4
  181.4 92.4 %copy-start.5 = (f32[1024,2,128]{0,2,1:T(8,128)S(1)}, f32[1024,2,128]{0,2,1:T(8,128)}, u32[]{:S(2)}) copy-start(f32[1024,2,128]{0,2,1:T(8,128)} %custom-call.1) | copy-start | bytes 3145732
  181.5 2.4 copy-start.6
  189.3 2.4 copy-start.6
  197.1 2.4 copy-start.6
  204.9 2.4 copy-start.6
  273.9 2.5 copy-start.3
  276.4 2.7 copy-start.7
  287.1 2.5 copy-start.3
  289.5 2.7 copy-start.7
  300.3 2.5 copy-start.3
  302.7 2.7 copy-start.7
  313.4 2.5 copy-start.3
  315.9 2.7 copy-start.7
  329.2 187.9 %all-reduce.4.cloned.1.call-start = ((), (), s32[]{:S(2)}) async-start(), calls=%async_computation.2 | async-start | bytes 8388608 | tf_op jit(solution)/shard_map/psum | solution.py:115
  329.2 85.2 %copy-start = (f32[2,1024,2,128]{3,2,1,0:T(2,128)S(1)}, f32[2,1024,2,128]{3,2,1,0:T(2,128)}, u32[]{:S(2)}) copy-start(f32[2,1024,2,128]{3,2,1,0:T(2,128)} %param.19) | copy-start | bytes 6291460
  411.5 3.0 copy-start.1
  411.5 3.0 copy-start.2
Sparse Core Ops, SparseCore 0:
  10.1 46.6 all-gather.4
  59.0 44.2 all-gather.6
  329.3 82.1 all-reduce.5
  414.7 102.2 all-reduce.3
where the time goes:
time: 527 us; the launch traced here: 525 us
  waiting for transfers between devices  265 us (50%)
  blocking collectives  97.6 us (19%)
  matrix products  87.3 us (17%)
  other arithmetic  33.9 us (6%)
  local copies, waits for them, and re-layouts  26.4 us (5%)
  between operations  13.9 us (3%)
    psum x1, waiting for transfers between devices, local(): summed = lax.psum(query_terms, 'slot')  94.6 us
    psum x1, waiting for transfers between devices, local(): key_total, value_total = lax.psum((key_grad, value_grad), 'conv')  81.8 us
    psum x1, blocking collectives, local(): row_sum = lax.psum(partial_sum, 'slot')  61.1 us
    all_gather x1, waiting for transfers between devices, local(): lax.all_gather(queries, 'slot', axis=0, tiled=True)  43.8 us
    all_gather x1, waiting for transfers between devices, local(): lax.all_gather(out_grad, 'slot', axis=0, tiled=True)  43.2 us
    all_gather x2, blocking collectives, merged(): everything = jax.tree.map(lambda part: lax.all_gather(part, axis), x)  36.5 us
    dot_general x8, matrix products, gradient_products(): jnp.einsum('rkgd,skd->rkgs', grad_block, value_half, preferred_element_ty...  32.8 us
    dot_general x12, matrix products, masked_scores(): jnp.einsum('rkgd,skd->rkgs', query_block, key_half, preferred_element_typ...  30.3 us
  transfers between devices with their start and end apart: 4, of which 4 were waited for; matrix products, arithmetic and copies ran while one was open for 4% of the time, Pallas kernels for 0%

commit v1 on v0

--- a/solution.py
+++ b/solution.py
@@ -112,7 +112,9 @@
         (query_blocks, grad_blocks, visible_all, log_total, row_sum),
     )
     query_terms = query_parts.reshape(total_rows, head_count, head_width)
-    summed = lax.psum(query_terms, "slot")
+    summed = query_terms
+    for hop in (1, 2, 4, 8):
+        summed = summed + lax.ppermute(summed, "slot", [(dev, dev ^ hop) for dev in range(16)])
     own_rows = queries.shape[0]
     query_grad = lax.dynamic_slice_in_dim(summed, lax.axis_index("slot") * own_rows, own_rows, 0)
     key_total, value_total = lax.psum((key_grad, value_grad), "conv")

time: 527 us -> 686 us (1.30)
  waiting for transfers between devices: 265 us -> 415 us
  other arithmetic: 33.9 us -> 42.9 us
    ppermute x0 -> x4, waiting for transfers between devices: none -> 211 us  [local(): lax.ppermute(summed, 'slot', [(dev, dev ^ hop) for dev in range(16)])]
    psum x1 -> x0, waiting for transfers between devices: 94.6 us -> none  [local(): summed = lax.psum(query_terms, 'slot')]
    psum x1, waiting for transfers between devices: 81.8 us -> 115 us  [local(): key_total, value_total = lax.psum((key_grad, value_grad), 'conv')]
    add x0 -> x4, other arithmetic: none -> 8.96 us  [local(): summed + lax.ppermute(summed, 'slot', [(dev, dev ^ hop) for dev in range(...]
  transfers between devices with their start and end apart: 4 -> 7, of which waited for: 4 -> 6; matrix products, arithmetic and copies ran while one was open for 4% -> 3% of each run, Pallas kernels for 0% -> 0%
where the time goes in v1:
time: 686 us; the launch traced here: 684 us
  waiting for transfers between devices  415 us (60%)
  blocking collectives  97.6 us (14%)
  matrix products  87.3 us (13%)
  other arithmetic  42.9 us (6%)
  local copies, waits for them, and re-layouts  24.7 us (4%)
  between operations  13.9 us (2%)
    ppermute x4, waiting for transfers between devices, local(): lax.ppermute(summed, 'slot', [(dev, dev ^ hop) for dev in range(16)])  211 us
    psum x1, waiting for transfers between devices, local(): key_total, value_total = lax.psum((key_grad, value_grad), 'conv')  115 us
    psum x1, blocking collectives, local(): row_sum = lax.psum(partial_sum, 'slot')  61.1 us
    all_gather x1, waiting for transfers between devices, local(): lax.all_gather(queries, 'slot', axis=0, tiled=True)  43.7 us
    all_gather x1, waiting for transfers between devices, local(): lax.all_gather(out_grad, 'slot', axis=0, tiled=True)  43.2 us
    all_gather x2, blocking collectives, merged(): everything = jax.tree.map(lambda part: lax.all_gather(part, axis), x)  36.5 us
    dot_general x8, matrix products, gradient_products(): jnp.einsum('rkgd,skd->rkgs', grad_block, value_half, preferred_element_ty...  32.8 us
    dot_general x12, matrix products, masked_scores(): jnp.einsum('rkgd,skd->rkgs', query_block, key_half, preferred_element_typ...  30.3 us
  transfers between devices with their start and end apart: 7, of which 6 were waited for; matrix products, arithmetic and copies ran while one was open for 3% of the time, Pallas kernels for 0%

profile of v1, /device:TPU:1, one launch (start us, length us, event | category | flops | bytes accessed | tf_op | source)
XLA Modules:
  0.0 684.2 jit_solution(293524422356822342)
XLA Ops:
  9.5 1.8 copy.70
  13.1 43.7 %all-gather.5.cloned.1.call-done = bf16[256,32,128]{2,1,0:T(8,128)(2,1)} async-done(((bf16[16,32,128]{2,1,0:T(8,128)(2,1)}), bf16[256,32,128]{2,1,0:T(8,128)(2,1)}) %all-gather.5.cloned.1.call-update) | async-done | bytes 2097168 | tf_op jit(solution)/shard_map/all_gather | solution.py:35
  56.9 3.3 copy.50
  60.1 43.2 %all-gather.7.cloned.1.call-done = bf16[256,32,128]{2,1,0:T(8,128)(2,1)} async-done(((bf16[16,32,128]{2,1,0:T(8,128)(2,1)}), bf16[256,32,128]{2,1,0:T(8,128)(2,1)}) %all-gather.7.cloned.1.call-update) | async-done | bytes 2097168 | tf_op jit(solution)/shard_map/all_gather | solution.py:36
  103.3 3.3 copy.51
  106.6 23.2 %while.54 = (s32[]{:T(128)}, f32[4,64,2,16]{1,3,2,0:T(8,128)S(1)}, f32[4,64,2,16]{1,3,2,0:T(8,128)S(1)}, pred[4,64,1024]{2,1,0:T(8,128)(4,1)S(1)}, bf16[4,64,2,1...) while((s32[]{:T(128)}, f32[4,64,2,16]{1,3,2,0:T(8,128)S(1)}, ...), condition=%wide.region_3.4_spmd, body=%wide.region_0.3_spmd.sunk | while | flops 553644032 | bytes 18210912 | solution.py:73
  106.6 2.8 bitcast_reduce_fusion.2
  109.4 2.8 fusion.87
  112.4 2.8 bitcast_reduce_fusion.2
  115.2 2.8 fusion.87
  118.2 2.8 bitcast_reduce_fusion.2
  121.0 2.8 fusion.87
  124.0 2.8 bitcast_reduce_fusion.2
  126.8 2.8 fusion.87
  129.8 19.1 %all-gather.1 = f32[64,64,2,16]{1,3,2,0:T(8,128)S(1)} all-gather(f32[4,64,2,16]{1,3,2,0:T(8,128)S(1)} %get-tuple-element.272), channel_id=3, replica_groups=mesh['slot'=16,'head'=2,'conv'=4] {'slot'}, dimensions={0}, use_global_device_ids=true | all-gather | bytes 557056 | tf_op jit(solution)/shard_map/all_gather | solution.py:16
  148.9 17.4 %all-gather = f32[64,64,2,16]{1,3,2,0:T(8,128)S(1)} all-gather(f32[4,64,2,16]{1,3,2,0:T(8,128)S(1)} %get-tuple-element.271), channel_id=2, replica_groups=mesh['slot'=16,'head'=2,'conv'=4] {'slot'}, dimensions={0}, use_global_device_ids=true | all-gather | bytes 557056 | tf_op jit(solution)/shard_map/all_gather | solution.py:16
  167.2 13.9 %while.55 = (s32[]{:T(128)}, f32[4,64,2,16]{1,3,2,0:T(8,128)S(1)}, f32[4,64,2,16]{1,3,2,0:T(8,128)S(1)}, f32[16,4,64,2,16]{2,4,3,1,0:T(8,128)}, f32[16,4,64,2,16...) while((s32[]{:T(128)}, f32[4,64,2,16]{1,3,2,0:T(8,128)S(1)}, f32[4,64,2,16]{1,3,2,0:T(8,128)S(1)}, ...), condition=%wide.region_5.6_spmd, body=%wide.region_4.5_spmd.sunk | while | flops 49157 | bytes 196731 | solution.py:22
  181.5 31.2 %while.56 = (s32[]{:T(128)}, f32[4,64,2,16]{3,1,2,0:T(8,128)}, pred[4,64,1024]{2,1,0:T(8,128)(4,1)S(1)}, bf16[4,64,2,16,128]{4,3,1,2,0:T(8,128)(2,1)}, bf16[1024...) while((s32[]{:T(128)}, f32[4,64,2,16]{3,1,2,0:T(8,128)}, ...), condition=%wide.region_8.9_spmd, body=%wide.region_6.8_spmd.sunk | while | flops 1086322688 | bytes 21397652 | solution.py:82
  181.5 2.4 fusion.93
  183.9 4.7 fusion.94
  189.4 2.4 fusion.93
  191.7 4.7 fusion.94
  197.1 2.4 fusion.93
  199.5 4.7 fusion.94
  204.9 2.4 fusion.93
  207.3 4.7 fusion.94
  212.7 61.1 %psum.21 = f32[4,64,2,16]{3,1,2,0:T(8,128)S(1)} all-reduce(f32[4,64,2,16]{3,1,2,0:T(8,128)} %get-tuple-element.275), channel_id=1, replica_groups=mesh['slot'=16,'head'=2,'conv'=4] {'slot'}, use_global_device_ids=true, to_apply=%region_9.10 | all-reduce | flops 8192 | bytes 65536 | tf_op jit(solution)/shard_map/psum | solution.py:83
  273.8 52.8 %while.57 = (s32[]{:T(128)}, f32[1024,2,128]{0,2,1:T(8,128)S(1)}, f32[1024,2,128]{0,2,1:T(8,128)S(1)}, f32[4,64,2,16,128]{4,3,2,1,0:T(8,128)}, bf16[4,64,2,16,12...) while((s32[]{:T(128)}, f32[1024,2,128]{0,2,1:T(8,128)S(1)}, ...), condition=%wide.region_11.12_spmd.clone, body=%wide.region_10.11_spmd.clone.sunk | while | flops 2711093248 | bytes 59867360 | solution.py:109
  273.9 2.4 fusion.105
  276.4 2.7 fusion.108
  279.1 3.5 fusion.106
  282.5 2.1 fusion.107
  284.7 1.2 fusion.109
  285.9 1.1 copy_dynamic-update-slice_fusion.2
  287.1 2.4 fusion.105
  289.6 2.7 fusion.108
  292.2 3.5 fusion.106
  295.7 2.1 fusion.107
  297.8 1.2 fusion.109
  299.1 1.2 copy_dynamic-update-slice_fusion.2
  300.3 2.4 fusion.105
  302.7 2.7 fusion.108
  305.4 3.5 fusion.106
  308.9 2.1 fusion.107
  311.0 1.2 fusion.109
  313.4 2.4 fusion.105
  315.9 2.7 fusion.108
  318.6 3.5 fusion.106
  322.1 2.1 fusion.107
  324.2 1.2 fusion.109
  325.4 1.2 copy_dynamic-update-slice_fusion.2
  326.6 65.7 %collective-permute-done = f32[256,32,128]{2,1,0:T(8,128)S(1)} collective-permute-done((f32[256,32,128]{2,1,0:T(8,128)}, f32[256,32,128]{2,1,0:T(8,128)S(1)}, u32[]{:S(2)}, u32[]{:S(2)}) %collective-permute-start) | collective-permute-done | bytes 4194336 | tf_op jit(solution)/shard_map/ppermute | solution.py:117
  392.3 3.2 add.100
  395.6 82.6 %collective-permute-done.1 = f32[256,32,128]{2,1,0:T(8,128)S(1)} collective-permute-done((f32[256,32,128]{2,1,0:T(8,128)S(1)}, f32[256,32,128]{2,1,0:T(8,128)S(1)}, u32[]{:S(2)}, u32[]{:S(2)}) %collective-permute-start.1) | collective-permute-done | bytes 4194336 | tf_op jit(solution)/shard_map/ppermute | solution.py:117
  479.4 62.9 %collective-permute-done.2 = f32[256,32,128]{2,1,0:T(8,128)S(1)} collective-permute-done((f32[256,32,128]{2,1,0:T(8,128)S(1)}, f32[256,32,128]{2,1,0:T(8,128)S(1)}, u32[]{:S(2)}, u32[]{:S(2)}) %collective-permute-start.2) | collective-permute-done | bytes 4194336 | tf_op jit(solution)/shard_map/ppermute | solution.py:117
  542.2 3.0 add.102
  545.2 2.2 collective-permute-start.3
  547.4 1.3 copy.52
  548.7 1.3 copy.53
  550.0 115.0 %all-reduce.3.cloned.1.call-done = (f32[1,1024,2,128]{3,2,1,0:T(2,128)}, f32[1,1024,2,128]{3,2,1,0:T(2,128)}) async-done(((f32[1,1024,2,128]{3,2,1,0:T(2,128)}, f32[1,1024,2,128]{3,2,1,0:T(2,128)}), (f32[1,1024,2,128]{3,2,1,0:T(2,128)}, f32[1,1024,2,128]{3,2,1,0:T(2,128)})) %all-reduce.3.cloned.1.call-update) | async-done | bytes 2097168 | tf_op jit(solution)/shard_map/psum | solution.py:120
  665.0 1.4 constant_dynamic-update-slice_fusion.3
  666.4 1.5 constant_dynamic-update-slice_fusion.2
  668.0 7.9 %divide_subtract_fusion = (f32[2,1024,2,128]{3,2,1,0:T(2,128)}, f32[2,1024,2,128]{3,2,1,0:T(2,128)}, f32[2,1024,2,128]{3,2,1,0:T(2,128)}) fusion(f32[2,1024,2,128]{3,2,1,0:T(2,128)S(1)} %copy-done, f32[2,1024,2,128]{3,2,1,0:T(2,128)S(1)} %constant_dynamic-update-slice_fusion.2, f32[2,1024,2,128]{3,2,1,0:T(2,128)S(1)} %copy-done.1, ...), kind=kLoop, calls=%fused_computation.80 | loop fusion | flops 6291456 | bytes 14680064 | tf_op jit(solution)/shard_map/sub | solution.py:126
  675.9 1.8 dynamic-slice_add_fusion
  (111 shorter events, 24.7 us)
Async XLA Ops:
  7.2 49.7 %all-gather.5.cloned.1.call-start = ((), (), s32[]{:S(2)}) async-start(), calls=%async_computation | async-start | bytes 2228224 | tf_op jit(solution)/shard_map/all_gather | solution.py:35
  7.9 95.4 %all-gather.7.cloned.1.call-start = ((), (), s32[]{:S(2)}) async-start(), calls=%async_computation.1 | async-start | bytes 2228224 | tf_op jit(solution)/shard_map/all_gather | solution.py:36
  8.6 656.3 %all-reduce.3.cloned.1.call-start = ((), (), s32[]{:S(2)}) async-start(), calls=%async_computation.2 | async-start | bytes 4194304 | tf_op jit(solution)/shard_map/psum | solution.py:120
  166.2 1.0 copy-start.4
  181.4 92.4 %copy-start.5 = (f32[1024,2,128]{0,2,1:T(8,128)S(1)}, f32[1024,2,128]{0,2,1:T(8,128)}, u32[]{:S(2)}) copy-start(f32[1024,2,128]{0,2,1:T(8,128)} %custom-call.1) | copy-start | bytes 3145732
  181.5 2.4 copy-start.6
  189.3 2.4 copy-start.6
  197.1 2.4 copy-start.6
  204.9 2.4 copy-start.6
  273.9 2.5 copy-start.3
  276.4 2.7 copy-start.7
  287.1 2.5 copy-start.3
  289.5 2.7 copy-start.7
  300.3 2.5 copy-start.3
  302.7 2.7 copy-start.7
  313.4 2.5 copy-start.3
  315.9 2.7 copy-start.7
  326.6 65.7 %collective-permute-start = (f32[256,32,128]{2,1,0:T(8,128)}, f32[256,32,128]{2,1,0:T(8,128)S(1)}, u32[]{:S(2)}, u32[]{:S(2)}) collective-permute-start(f32[256,32,128]{2,1,0:T(8,128)} %bitcast.229), channel_id=1, source_target_pairs={{0,8},{8,0},{16,24},{24,16},{32,40},{40,32},{48,56},{56,48},{64,72... | collective-permute-start | bytes 12582920 | tf_op jit(solution)/shard_map/ppermute | solution.py:117
  395.5 82.7 %collective-permute-start.1 = (f32[256,32,128]{2,1,0:T(8,128)S(1)}, f32[256,32,128]{2,1,0:T(8,128)S(1)}, u32[]{:S(2)}, u32[]{:S(2)}) collective-permute-start(f32[256,32,128]{2,1,0:T(8,128)S(1)} %add.100), channel_id=1, source_target_pairs={{0,16},{8,24},{16,0},{24,8},{32,48},{40,56},{48,32},{56,40},{64,80... | collective-permute-start | bytes 12582920 | tf_op jit(solution)/shard_map/ppermute | solution.py:117
  479.3 63.0 %collective-permute-start.2 = (f32[256,32,128]{2,1,0:T(8,128)S(1)}, f32[256,32,128]{2,1,0:T(8,128)S(1)}, u32[]{:S(2)}, u32[]{:S(2)}) collective-permute-start(f32[256,32,128]{2,1,0:T(8,128)S(1)} %add.101), channel_id=1, source_target_pairs={{0,32},{8,40},{16,48},{24,56},{32,0},{40,8},{48,16},{56,24},{64,96... | collective-permute-start | bytes 12582920 | tf_op jit(solution)/shard_map/ppermute | solution.py:117
  545.2 130.7 %collective-permute-start.3 = (f32[256,32,128]{2,1,0:T(8,128)}, f32[256,32,128]{2,1,0:T(8,128)}, u32[]{:S(2)}, u32[]{:S(2)}) collective-permute-start(f32[256,32,128]{2,1,0:T(8,128)} %add.102), channel_id=1, source_target_pairs={{0,64},{8,72},{16,80},{24,88},{32,96},{40,104},{48,112},{56,120},{... | collective-permute-start | bytes 12582920 | tf_op jit(solution)/shard_map/ppermute | solution.py:117
  548.7 119.3 %copy-start = (f32[2,1024,2,128]{3,2,1,0:T(2,128)S(1)}, f32[2,1024,2,128]{3,2,1,0:T(2,128)}, u32[]{:S(2)}) copy-start(f32[2,1024,2,128]{3,2,1,0:T(2,128)} %param.19) | copy-start | bytes 6291460
  665.0 3.0 copy-start.1
  665.0 3.0 copy-start.2
Sparse Core Ops, SparseCore 0:
  10.1 46.6 all-gather.4
  59.0 44.2 all-gather.6
  550.1 114.8 all-reduce.2
